TPU v7x, 32 devices: a whole 2x2x4 slice. The times are simulated.
32 devices in a mesh: fsdp: 4 (over z), adapter: 8 (over y, x, core).
Axes of the slice: x: 2, y: 2, z: 4, core: 2. Of those that a mesh axis runs over, the one named last changes fastest.
Arguments:
- tokens: bfloat16 [2048, 8192], P('adapter', 'fsdp'), may hold values from -6 to 6
- tenant: int32 [2048], P('adapter'), may hold values from 0 to 63, as said below
- send_list: int32 [8, 8, 128], P('adapter'), may hold values from -1 to 255, as said below
- base_weight: bfloat16 [8192, 2048], P('fsdp'), may hold values from -0.09375 to 0.09375
- down_weight: bfloat16 [64, 8192, 128], P('adapter', 'fsdp'), may hold values from -0.0625 to 0.0625
- up_projection_weight: bfloat16 [64, 64, 2048], P('adapter', None, 'fsdp'), may hold values from -0.75 to 0.75
- cotangent: bfloat16 [2048, 2048], P('adapter', 'fsdp'), may hold values from -3 to 3
Outputs:
- projected: bfloat16 [2048, 2048], P('adapter', 'fsdp')
- token_gradient: bfloat16 [2048, 8192], P('adapter', 'fsdp')
- down_weight_gradient: bfloat16 [64, 8192, 128], P('adapter', 'fsdp')
- up_weight_gradient: bfloat16 [64, 64, 2048], P('adapter', None, 'fsdp')
Inputs may be any that keep to these rules, and one draw needn't show every extreme that they name: `tenant`: adapter t belongs to owner t // 8. Among the 256 rows of one index of adapter at most 128 belong to the adapters of one owner, and one owner, the same for every index, has exactly 128 of them. send_list[i, o, :] lists in increasing order the rows (numbered within the 256 rows of index i of adapter) whose tenant belongs to owner o, then -1 in the slots left; every row stands in exactly one list.
All inputs are finite; a program needn't handle non-finite values.
Results may differ from a plain program's by a relative error of at most 0.005.
Values may be sent and summed in bfloat16 or wider, within the bound.
No kernel may reach another device: no remote copies, remote signals or barrier semaphores. Data moves between devices by JAX's collectives and lax.ppermute only.
A program may use at most 128 MiB of HBM per device.

v0:
```python
import jax
import jax.numpy as jnp
from jax import lax
from jax.sharding import PartitionSpec as P

KV = 1024
adapter_scale = 0.5


def down_partial(input_rows, weights_f, down_weight):
    low_all = jnp.einsum("sd,ldk->slk", input_rows, down_weight, preferred_element_type=jnp.float32)
    return jnp.sum(low_all * weights_f[:, :, None], axis=1)


def grad_partial(rows_dy, weights_f, up_projection_weight, selected_half):
    rank_size = up_projection_weight.shape[1]
    back_all = jnp.einsum(
        "sc,lrc->slr", rows_dy, up_projection_weight, preferred_element_type=jnp.float32
    )
    half_sum = jnp.sum(back_all * weights_f[:, :, None], axis=1)
    placed = jnp.zeros((rows_dy.shape[0], 2 * rank_size), jnp.float32)
    zero_idx = jnp.zeros((), jnp.int32)
    return lax.dynamic_update_slice(placed, half_sum, (zero_idx, selected_half * rank_size))


def forward_holder(low_rank, weight_table, up_projection_weight, selected_half):
    rank_size = up_projection_weight.shape[1]
    low_half = lax.dynamic_slice_in_dim(low_rank, selected_half * rank_size, rank_size, 1)
    broadcast_rows = low_half[:, None, :] * weight_table[:, :, None]
    adapter_update = adapter_scale * jnp.einsum(
        "slr,lrc->sc", broadcast_rows, up_projection_weight, preferred_element_type=jnp.float32
    )
    return (adapter_update.astype(jnp.bfloat16), broadcast_rows)


def backward_owner(back_low, weight_table, input_rows, rows_dy, broadcast_rows, down_weight):
    widened_rows = back_low[:, None, :] * weight_table[:, :, None]
    backward_update = adapter_scale * jnp.einsum(
        "wnr,nyr->wy", widened_rows, down_weight, preferred_element_type=jnp.float32
    )
    down_weight_gradient = adapter_scale * jnp.einsum(
        "wq,wmu->mqu", input_rows, widened_rows, preferred_element_type=jnp.float32
    )
    up_weight_gradient = adapter_scale * jnp.einsum(
        "slr,sc->lrc", broadcast_rows, rows_dy, preferred_element_type=jnp.float32
    )
    return (
        backward_update.astype(jnp.bfloat16),
        down_weight_gradient.astype(jnp.bfloat16),
        up_weight_gradient.astype(jnp.bfloat16),
    )


def shards(tokens, tenant, send_list, base_weight, down_weight, up_projection_weight, cotangent):
    rows_here = tokens.shape[0]
    width_here = tokens.shape[1]
    column_span = cotangent.shape[1]
    adapters_here = down_weight.shape[0]
    holder_list = send_list.shape[1]
    slot_capacity = send_list.shape[2]
    total_slots = holder_list * slot_capacity
    listed = send_list[0]
    present = listed >= 0
    safe_rows = jnp.where(present, listed, 0)
    local_ids = tenant % adapters_here
    picked_ids = local_ids[safe_rows]
    adapter_ids = jnp.arange(adapters_here, dtype=jnp.int32)
    selector = (
        (picked_ids[:, :, None] == adapter_ids[None, None, :]) & present[:, :, None]
    ).astype(jnp.bfloat16)
    send_x = tokens[safe_rows]
    send_dy = cotangent[safe_rows]
    drop_rows = jnp.where(present, listed, rows_here).reshape(total_slots)
    fsdp_pos = lax.axis_index("fsdp")
    selected_half = fsdp_pos * column_span // KV
    weight_cols = base_weight
    local_base_output = lax.psum_scatter(
        lax.dot_general(
            weight_cols, tokens, (((0,), (1,)), ((), ())), preferred_element_type=jnp.float32
        ),
        "fsdp",
        scatter_dimension=0,
        tiled=True,
    ).T
    weight_cols = base_weight
    input_frozen_part = lax.dot_general(
        lax.all_gather(cotangent, "fsdp", axis=1, tiled=True),
        weight_cols,
        (((1,), (1,)), ((), ())),
        preferred_element_type=jnp.float32,
    )
    recv_x, recv_sel = (
        lax.all_to_all(send_x, "adapter", split_axis=0, concat_axis=0, tiled=True),
        lax.all_to_all(selector, "adapter", split_axis=0, concat_axis=0, tiled=True),
    )
    input_rows = recv_x.reshape(total_slots, width_here)
    weight_table = recv_sel.reshape(total_slots, adapters_here)
    weights_f = weight_table.astype(jnp.float32)
    low_term = down_partial(input_rows, weights_f, down_weight)
    reduced_rank_sum = lax.psum(low_term, "fsdp")
    adapter_update, broadcast_rows = forward_holder(
        reduced_rank_sum.astype(jnp.bfloat16), weight_table, up_projection_weight, selected_half
    )
    got_delta = lax.all_to_all(
        adapter_update.reshape(holder_list, slot_capacity, column_span),
        "adapter",
        split_axis=0,
        concat_axis=0,
        tiled=True,
    )
    recv_dy = lax.all_to_all(send_dy, "adapter", split_axis=0, concat_axis=0, tiled=True)
    rows_dy = recv_dy.reshape(total_slots, column_span)
    back_sum = lax.psum(
        grad_partial(rows_dy, weights_f, up_projection_weight, selected_half), "fsdp"
    )
    backward_update, down_weight_gradient, up_weight_gradient = backward_owner(
        back_sum.astype(jnp.bfloat16),
        weight_table,
        input_rows,
        rows_dy,
        broadcast_rows,
        down_weight,
    )
    got_back = lax.all_to_all(
        backward_update.reshape(holder_list, slot_capacity, width_here),
        "adapter",
        split_axis=0,
        concat_axis=0,
        tiled=True,
    )
    adapter_columns = (
        jnp.zeros((rows_here, column_span), jnp.float32)
        .at[drop_rows]
        .add(got_delta.reshape(total_slots, column_span).astype(jnp.float32), mode="drop")
    )
    projected = (local_base_output + adapter_columns).astype(jnp.bfloat16)
    adapter_backward = (
        jnp.zeros((rows_here, width_here), jnp.float32)
        .at[drop_rows]
        .add(got_back.reshape(total_slots, width_here).astype(jnp.float32), mode="drop")
    )
    token_gradient = (input_frozen_part + adapter_backward).astype(jnp.bfloat16)
    return (projected, token_gradient, down_weight_gradient, up_weight_gradient)


def solution(mesh):
    in_specs = (
        P("adapter", "fsdp"),
        P("adapter"),
        P("adapter", None, None),
        P("fsdp", None),
        P("adapter", "fsdp", None),
        P("adapter", None, "fsdp"),
        P("adapter", "fsdp"),
    )
    out_specs = (
        P("adapter", "fsdp"),
        P("adapter", "fsdp"),
        P("adapter", "fsdp", None),
        P("adapter", None, "fsdp"),
    )
    return jax.shard_map(shards, mesh=mesh, in_specs=in_specs, out_specs=out_specs, check_vma=False)
```

profile of v0, /device:TPU:0, one launch (start us, length us, event | category | flops | bytes accessed | tf_op | source)
XLA Modules:
  0.0 267.3 jit_solution(12076343468223439721)
XLA Ops:
  7.2 0.0 copy-start
  7.2 0.0 copy-start.1
  7.2 0.8 fusion.29
  8.0 0.7 compare_bitcast_fusion
  8.7 0.7 and_select_fusion
  9.4 6.8 %gather_fusion.1 = s32[1024]{0:T(1024)S(1)} fusion(s32[256]{0:T(256)S(1)} %and_select_fusion, s32[1024]{0:T(1024)S(1)} %fusion.29), kind=kCustom, calls=%fused_computation.1 | custom fusion | bytes 12288 | tf_op jit(solution)/shard_map/gather | solution.py:66
  16.2 0.6 fusion.27
  16.8 5.2 %all-to-all-start.1 = ((bf16[8,128,8]{1,2,0:T(8,128)(2,1)}), bf16[8,128,8]{1,2,0:T(8,128)(2,1)S(1)}, u32[]{:S(2)}, u32[]{:S(2)}) async-start(bf16[8,128,8]{1,2,0:T(8,128)(2,1)} %fusion.27), calls=%async_computation.2 | async-start | bytes 32768 | tf_op jit(solution)/shard_map/all_to_all | solution.py:94
  22.0 0.0 copy-done.1
  22.0 5.1 %gather_fusion.2 = bf16[1024,512]{1,0:T(8,128)(2,1)} fusion(bf16[256,512]{1,0:T(8,128)(2,1)S(1)} %copy-done.1, s32[1024]{0:T(1024)S(1)} %fusion.29), kind=kCustom, calls=%fused_computation.2 | custom fusion | bytes 2101248 | tf_op jit(solution)/shard_map/gather | solution.py:72
  27.1 0.0 all-to-all-done.1
  27.1 4.2 %all-to-all-start.3 = ((bf16[8,128,512]{2,1,0:T(8,128)(2,1)}), bf16[8,128,512]{2,1,0:T(8,128)(2,1)S(1)}, u32[]{:S(2)}, u32[]{:S(2)}) async-start(bf16[8,128,512]{2,1,0:T(8,128)(2,1)} %bitcast.14), calls=%async_computation.4 | async-start | bytes 2097152 | tf_op jit(solution)/shard_map/all_to_all | solution.py:111
  31.3 0.0 copy-done
  31.3 6.0 %gather_fusion = bf16[1024,2048]{1,0:T(8,128)(2,1)} fusion(bf16[256,2048]{1,0:T(8,128)(2,1)S(1)} %copy-done, s32[1024]{0:T(1024)S(1)} %fusion.29), kind=kCustom, calls=%fused_computation | custom fusion | bytes 8392704 | tf_op jit(solution)/shard_map/gather | solution.py:71
  37.2 9.4 %all-to-all-done.3 = bf16[8,128,512]{2,1,0:T(8,128)(2,1)S(1)} async-done(((bf16[8,128,512]{2,1,0:T(8,128)(2,1)}), bf16[8,128,512]{2,1,0:T(8,128)(2,1)S(1)}, u32[]{:S(2)}, u32[]{:S(2)}) %all-to-all-start.3) | async-done | bytes 1048608 | tf_op jit(solution)/shard_map/all_to_all | solution.py:111
  46.7 4.6 %all-to-all-start = ((bf16[8,128,2048]{2,1,0:T(8,128)(2,1)}), bf16[8,128,2048]{2,1,0:T(8,128)(2,1)}, u32[]{:S(2)}, u32[]{:S(2)}) async-start(bf16[8,128,2048]{2,1,0:T(8,128)(2,1)} %bitcast.50), calls=%async_computation.1 | async-start | bytes 8388608 | tf_op jit(solution)/shard_map/all_to_all | solution.py:93
  51.3 0.0 all-gather.2.cloned.1.call-start
  51.3 0.7 all-gather.2.cloned.1.call-update
  52.0 0.0 copy-start.3
  52.0 0.0 reduce-scatter.2.cloned.1.call-start
  52.1 7.2 %fusion.31 = f32[2048,256]{1,0:T(8,128)} fusion(bf16[2048,2048]{1,0:T(8,128)(2,1)} %param.10, bf16[256,2048]{1,0:T(8,128)(2,1)S(1)} %copy-done), kind=kOutput, calls=%fused_computation.49 | convolution fusion | flops 2147483648 | bytes 11534336 | tf_op jit(solution)/shard_map/dot_general | solution.py:78
  59.3 0.0 reduce-scatter.2.cloned.1.call-update
  59.3 0.0 copy-done.3
  59.4 0.7 multiply_reduce_fusion.1
  60.2 40.2 %all-to-all-done = bf16[8,128,2048]{2,1,0:T(8,128)(2,1)} async-done(((bf16[8,128,2048]{2,1,0:T(8,128)(2,1)}), bf16[8,128,2048]{2,1,0:T(8,128)(2,1)}, u32[]{:S(2)}, u32[]{:S(2)}) %all-to-all-start) | async-done | bytes 4194336 | tf_op jit(solution)/shard_map/all_to_all | solution.py:93
  100.4 7.6 %multiply_reduce_fusion = f32[1024,128]{1,0:T(8,128)S(1)} fusion(bf16[1024,2048,1]{1,0,2:T(8,128)(2,1)} %bitcast.7, bf16[8,2048,128]{2,1,0:T(8,128)(2,1)} %param.11, f32[1024,8]{0,1:T(8,128)S(1)} %bitcast_convert_fusion), kind=kOutput, calls=%fused_computation.10 | convolution fusion | flops 4296933376 | bytes 8945664 | tf_op jit(solution)/shard_map/sd,ldk->slk/dot_general | solution.py:11
  107.9 56.5 %all-reduce.2 = (bf16[1024,128]{1,0:T(8,128)(2,1)S(1)}, bf16[1024,128]{0,1:T(8,128)(2,1)}) all-reduce(f32[1024,128]{1,0:T(8,128)S(1)} %multiply_reduce_fusion, f32[1024,128]{0,1:T(8,128)S(1)} %constant_dynamic-update-slice_fusion), channel_id=1, replica_groups=mesh['fsdp'=4,'adapter'=8] {'fsdp'}, use_global_device_ids=true, to_apply=%region_2.3 | all-reduce | flops 262144 | bytes 1572864 | tf_op jit(solution)/shard_map/psum | solution.py:100
  164.4 0.1 dynamic-slice_convert_fusion
  164.5 0.1 copy.17
  164.7 2.8 %fusion.8 = bf16[1024,512]{1,0:T(8,128)(2,1)} fusion(bf16[8,64,512]{2,1,0:T(8,128)(2,1)} %param.12, bf16[1024,8]{0,1:T(8,128)(2,1)S(1)} %bitcast.57, bf16[1024,64]{0,1:T(8,128)(2,1)S(1)} %copy.17), kind=kOutput, calls=%fused_computation.17 | convolution fusion | flops 538443776 | bytes 1720320 | tf_op jit(solution)/shard_map/slr,lrc->sc/dot_general | solution.py:30
  167.4 3.6 %all-to-all-start.2 = ((bf16[8,128,512]{2,1,0:T(8,128)(2,1)}), bf16[8,128,512]{2,1,0:T(8,128)(2,1)S(1)}, u32[]{:S(2)}, u32[]{:S(2)}) async-start(bf16[8,128,512]{2,1,0:T(8,128)(2,1)} %bitcast.55), calls=%async_computation.3 | async-start | bytes 2097152 | tf_op jit(solution)/shard_map/all_to_all | solution.py:104
  171.0 8.4 %fusion.2 = bf16[1024,2048]{1,0:T(8,128)(2,1)} fusion(bf16[8,2048,128]{2,1,0:T(8,128)(2,1)} %param.11, bf16[1024,8]{0,1:T(8,128)(2,1)S(1)} %bitcast.58, bf16[1024,128]{0,1:T(8,128)(2,1)} %get-tuple-element.17), kind=kOutput, calls=%fused_computation.8 | convolution fusion | flops 4300210176 | bytes 8667136 | tf_op jit(solution)/shard_map/wnr,nyr->wy/dot_general | solution.py:38
  179.4 7.0 %all-to-all-done.2 = bf16[8,128,512]{2,1,0:T(8,128)(2,1)S(1)} async-done(((bf16[8,128,512]{2,1,0:T(8,128)(2,1)}), bf16[8,128,512]{2,1,0:T(8,128)(2,1)S(1)}, u32[]{:S(2)}, u32[]{:S(2)}) %all-to-all-start.2) | async-done | bytes 1048608 | tf_op jit(solution)/shard_map/all_to_all | solution.py:104
  186.5 4.9 %all-to-all-start.4 = ((bf16[8,128,2048]{2,1,0:T(8,128)(2,1)}), bf16[8,128,2048]{2,1,0:T(8,128)(2,1)}, u32[]{:S(2)}, u32[]{:S(2)}) async-start(bf16[8,128,2048]{2,1,0:T(8,128)(2,1)} %bitcast.51), calls=%async_computation.5 | async-start | bytes 8388608 | tf_op jit(solution)/shard_map/all_to_all | solution.py:124
  191.3 0.0 copy-done.2
  191.4 0.0 all-gather.2.cloned.1.call-done
  191.4 0.0 copy-start.4
  191.4 7.4 %fusion.32 = f32[256,2048]{1,0:T(8,128)} fusion(bf16[256,2048]{1,0:T(8,128)(2,1)} %all-gather.2.cloned.1.call-done, bf16[2048,2048]{1,0:T(8,128)(2,1)} %param.10), kind=kOutput, calls=%fused_computation.50 | convolution fusion | flops 2147483648 | bytes 11534336 | tf_op jit(solution)/shard_map/dot_general | solution.py:86
  198.8 0.0 copy-done.4
  198.8 8.2 %fusion.3 = bf16[8,2048,128]{1,2,0:T(8,128)(2,1)} fusion(bf16[1024,2048,1]{1,0,2:T(8,128)(2,1)} %bitcast.7, bf16[1024,8]{0,1:T(8,128)(2,1)S(1)} %bitcast.59, bf16[1024,128]{0,1:T(8,128)(2,1)S(1)} %copy-done.4), kind=kOutput, calls=%fused_computation.11 | convolution fusion | flops 4300210176 | bytes 8667136 | tf_op jit(solution)/shard_map/wq,wmu->mqu/dot_general | solution.py:41
  207.1 6.4 %copy.20 = bf16[8,2048,128]{2,1,0:T(8,128)(2,1)} copy(bf16[8,2048,128]{1,2,0:T(8,128)(2,1)} %fusion.3) | data formatting | bytes 8388608
  213.5 1.5 fusion.15
  215.0 1.2 copy.18
  216.2 7.2 %scatter_custom_fusion = f32[256,512]{1,0:T(8,128)S(1)} fusion(f32[256,512]{1,0:T(8,128)S(1)} %copy.18, s32[1024]{0:T(1024)S(1)} %bitcast.63, bf16[1024,512]{1,0:T(8,128)(2,1)S(1)} %bitcast.52), kind=kCustom, calls=%fused_computation.14 | custom fusion | flops 1048576 | bytes 1572864 | tf_op jit(solution)/shard_map/scatter-add | solution.py:134
  223.4 0.7 convert_element_type.55
  224.1 16.1 %all-to-all-done.4 = bf16[8,128,2048]{2,1,0:T(8,128)(2,1)} async-done(((bf16[8,128,2048]{2,1,0:T(8,128)(2,1)}), bf16[8,128,2048]{2,1,0:T(8,128)(2,1)}, u32[]{:S(2)}, u32[]{:S(2)}) %all-to-all-start.4) | async-done | bytes 4194336 | tf_op jit(solution)/shard_map/all_to_all | solution.py:124
  240.3 17.5 %scatter_custom_fusion.1 = f32[256,2048]{1,0:T(8,128)} fusion(f32[256,2048]{1,0:T(8,128)} %fusion.32, s32[1024]{0:T(1024)S(1)} %bitcast.64, bf16[1024,2048]{1,0:T(8,128)(2,1)} %bitcast.24), kind=kCustom, calls=%fused_computation.5 | custom fusion | flops 4194304 | bytes 6291456 | tf_op jit(solution)/shard_map/scatter-add | solution.py:140
  257.8 2.7 %convert_element_type.60 = bf16[256,2048]{1,0:T(8,128)(2,1)} convert(f32[256,2048]{1,0:T(8,128)} %scatter_custom_fusion.1) | non-fusion elementwise | flops 524288 | bytes 3145728 | tf_op jit(solution)/shard_map/convert_element_type | solution.py:142
  (6 shorter events, 0.1 us)
Async XLA Ops:
  7.2 24.1 %copy-start = (bf16[256,2048]{1,0:T(8,128)(2,1)S(1)}, bf16[256,2048]{1,0:T(8,128)(2,1)}, u32[]{:S(2)}) copy-start(bf16[256,2048]{1,0:T(8,128)(2,1)} %param.7) | copy-start | bytes 3145732
  7.2 14.8 %copy-start.1 = (bf16[256,512]{1,0:T(8,128)(2,1)S(1)}, bf16[256,512]{1,0:T(8,128)(2,1)}, u32[]{:S(2)}) copy-start(bf16[256,512]{1,0:T(8,128)(2,1)} %param.13) | copy-start | bytes 786436
  16.8 10.3 %all-to-all-start.1 = ((bf16[8,128,8]{1,2,0:T(8,128)(2,1)}), bf16[8,128,8]{1,2,0:T(8,128)(2,1)S(1)}, u32[]{:S(2)}, u32[]{:S(2)}) async-start(bf16[8,128,8]{1,2,0:T(8,128)(2,1)} %fusion.27), calls=%async_computation.2 | async-start | bytes 32768 | tf_op jit(solution)/shard_map/all_to_all | solution.py:94
  27.1 19.6 %all-to-all-start.3 = ((bf16[8,128,512]{2,1,0:T(8,128)(2,1)}), bf16[8,128,512]{2,1,0:T(8,128)(2,1)S(1)}, u32[]{:S(2)}, u32[]{:S(2)}) async-start(bf16[8,128,512]{2,1,0:T(8,128)(2,1)} %bitcast.14), calls=%async_computation.4 | async-start | bytes 2097152 | tf_op jit(solution)/shard_map/all_to_all | solution.py:111
  46.7 53.7 %all-to-all-start = ((bf16[8,128,2048]{2,1,0:T(8,128)(2,1)}), bf16[8,128,2048]{2,1,0:T(8,128)(2,1)}, u32[]{:S(2)}, u32[]{:S(2)}) async-start(bf16[8,128,2048]{2,1,0:T(8,128)(2,1)} %bitcast.50), calls=%async_computation.1 | async-start | bytes 8388608 | tf_op jit(solution)/shard_map/all_to_all | solution.py:93
  51.3 140.1 %all-gather.2.cloned.1.call-start = ((), (), s32[]{:S(2)}) async-start(), calls=%async_computation.7 | async-start | bytes 1310720 | tf_op jit(solution)/shard_map/all_gather | solution.py:87
  52.0 7.3 %copy-start.3 = (bf16[8,64,512]{2,1,0:T(8,128)(2,1)S(1)}, bf16[8,64,512]{2,1,0:T(8,128)(2,1)}, u32[]{:S(2)}) copy-start(bf16[8,64,512]{2,1,0:T(8,128)(2,1)} %param.12) | copy-start | bytes 1572868
  52.0 163.0 %reduce-scatter.2.cloned.1.call-start = ((), (), s32[]{:S(2)}) async-start(), calls=%async_computation.6 | async-start | bytes 2621440 | tf_op jit(solution)/shard_map/reduce_scatter | solution.py:77
  167.4 19.0 %all-to-all-start.2 = ((bf16[8,128,512]{2,1,0:T(8,128)(2,1)}), bf16[8,128,512]{2,1,0:T(8,128)(2,1)S(1)}, u32[]{:S(2)}, u32[]{:S(2)}) async-start(bf16[8,128,512]{2,1,0:T(8,128)(2,1)} %bitcast.55), calls=%async_computation.3 | async-start | bytes 2097152 | tf_op jit(solution)/shard_map/all_to_all | solution.py:104
  186.5 4.9 %copy-start.2 = (s32[1,8,128]{2,1,0:T(8,128)S(1)}, s32[1,8,128]{2,1,0:T(8,128)}, u32[]{:S(2)}) copy-start(s32[1,8,128]{2,1,0:T(8,128)} %param.9) | copy-start | bytes 12292
  186.5 53.8 %all-to-all-start.4 = ((bf16[8,128,2048]{2,1,0:T(8,128)(2,1)}), bf16[8,128,2048]{2,1,0:T(8,128)(2,1)}, u32[]{:S(2)}, u32[]{:S(2)}) async-start(bf16[8,128,2048]{2,1,0:T(8,128)(2,1)} %bitcast.51), calls=%async_computation.5 | async-start | bytes 8388608 | tf_op jit(solution)/shard_map/all_to_all | solution.py:124
  191.4 7.5 %copy-start.4 = (bf16[1024,128]{0,1:T(8,128)(2,1)S(1)}, bf16[1024,128]{0,1:T(8,128)(2,1)}, u32[]{:S(2)}) copy-start(bf16[1024,128]{0,1:T(8,128)(2,1)} %get-tuple-element.17) | copy-start | bytes 786436
Sparse Core Ops, SparseCore 0:
  53.7 29.5 all-gather.1
  85.5 58.0 reduce-scatter.1
where the time goes:
time: 268 us; the launch traced here: 267 us
  waiting for transfers between devices  73.5 us (27%)
  blocking collectives  56.5 us (21%)
  matrix products  43.9 us (16%)
  other arithmetic  30.9 us (12%)
  local copies, waits for them, and re-layouts  25.9 us (10%)
  starting transfers between devices  22.5 us (8%)
  between operations  14.2 us (5%)
    psum x1, blocking collectives, shards(): reduced_rank_sum = lax.psum(low_term, 'fsdp')  56.5 us
    all_to_all x1, waiting for transfers between devices, shards(): lax.all_to_all(send_x, 'adapter', split_axis=0, concat_axis=0, tiled=True)  40.2 us
    scatter-add x1, other arithmetic, shards(): adapter_backward = jnp.zeros((rows_here, width_here), jnp.float32).at[dro...  17.5 us
    all_to_all x1, waiting for transfers between devices, shards(): lax.all_to_all(backward_update.reshape(holder_list, slot_capacity, width_...  16.1 us
    all_to_all x1, waiting for transfers between devices, shards(): lax.all_to_all(send_dy, 'adapter', split_axis=0, concat_axis=0, tiled=True)  9.44 us
    dot_general x1, matrix products, backward_owner(): jnp.einsum('wnr,nyr->wy', widened_rows, down_weight, preferred_element_ty...  8.41 us
    dot_general x1, matrix products, backward_owner(): jnp.einsum('wq,wmu->mqu', input_rows, widened_rows, preferred_element_typ...  8.22 us
    dot_general x1, matrix products, down_partial(): jnp.einsum('sd,ldk->slk', input_rows, down_weight, preferred_element_type...  7.56 us
  transfers between devices with their start and end apart: 7, of which 4 were waited for; matrix products, arithmetic and copies ran while one was open for 26% of the time, Pallas kernels for 0%

commit v1 on v0

--- a/solution.py
+++ b/solution.py
@@ -5,6 +5,15 @@
 
 KV = 1024
 adapter_scale = 0.5
+
+
+def sum_by_hops(x, name):
+    peers = lax.axis_size(name)
+    acc, far = (x, 1)
+    while far < peers:
+        acc = acc + lax.ppermute(acc, name, [(i, i ^ far) for i in range(peers)])
+        far = 2 * far
+    return acc
 
 
 def down_partial(input_rows, weights_f, down_weight):
@@ -97,7 +106,7 @@
     weight_table = recv_sel.reshape(total_slots, adapters_here)
     weights_f = weight_table.astype(jnp.float32)
     low_term = down_partial(input_rows, weights_f, down_weight)
-    reduced_rank_sum = lax.psum(low_term, "fsdp")
+    reduced_rank_sum = sum_by_hops(low_term, "fsdp")
     adapter_update, broadcast_rows = forward_holder(
         reduced_rank_sum.astype(jnp.bfloat16), weight_table, up_projection_weight, selected_half
     )

time: 268 us -> 248 us (0.925)
  blocking collectives: 56.5 us -> 40.8 us
  waiting for transfers between devices: 73.5 us -> 68.8 us
    ppermute x0 -> x2, waiting for transfers between devices: none -> 58.6 us  [sum_by_hops(): acc = acc + lax.ppermute(acc, name, [(i, i ^ far) for i in range(peers)])]
    all_to_all x1, waiting for transfers between devices: 40.2 us -> 0.01 us  [shards(): lax.all_to_all(send_x, 'adapter', split_axis=0, concat_axis=0, tiled=True)]
    all_to_all x1, waiting for transfers between devices: 16.1 us -> 0.01 us  [shards(): lax.all_to_all(backward_update.reshape(holder_list, slot_capacity, width_...]
    psum x1, blocking collectives: 56.5 us -> 40.8 us  [shards(): lax.psum(grad_partial(rows_dy, weights_f, up_projection_weight, selected_...]
    all_to_all x1, waiting for transfers between devices: 7 us -> 0.01 us  [shards(): lax.all_to_all(adapter_update.reshape(holder_list, slot_capacity, column_...]
  transfers between devices with their start and end apart: 7 -> 9, of which waited for: 4 -> 3; matrix products, arithmetic and copies ran while one was open for 26% -> 34% of each run, Pallas kernels for 0% -> 0%
where the time goes in v1:
time: 248 us
  waiting for transfers between devices  68.8 us (28%)
  matrix products  44.1 us (18%)
  blocking collectives  40.8 us (16%)
  other arithmetic  31.1 us (13%)
  local copies, waits for them, and re-layouts  25.8 us (10%)
  starting transfers between devices  22.8 us (9%)
  between operations  14.3 us (6%)
    ppermute x2, waiting for transfers between devices, sum_by_hops(): acc = acc + lax.ppermute(acc, name, [(i, i ^ far) for i in range(peers)])  58.6 us
    psum x1, blocking collectives, shards(): lax.psum(grad_partial(rows_dy, weights_f, up_projection_weight, selected_...  40.8 us
    scatter-add x1, other arithmetic, shards(): adapter_backward = jnp.zeros((rows_here, width_here), jnp.float32).at[dro...  17.5 us
    all_to_all x1, waiting for transfers between devices, shards(): lax.all_to_all(send_dy, 'adapter', split_axis=0, concat_axis=0, tiled=True)  9.44 us
    dot_general x1, matrix products, backward_owner(): jnp.einsum('wnr,nyr->wy', widened_rows, down_weight, preferred_element_ty...  8.35 us
    dot_general x1, matrix products, backward_owner(): jnp.einsum('wq,wmu->mqu', input_rows, widened_rows, preferred_element_typ...  8.23 us
    dot_general x1, matrix products, down_partial(): jnp.einsum('sd,ldk->slk', input_rows, down_weight, preferred_element_type...  7.58 us
    dot_general x1, matrix products, shards(): lax.dot_general(lax.all_gather(cotangent, 'fsdp', axis=1, tiled=True), we...  7.46 us
  transfers between devices with their start and end apart: 9, of which 3 were waited for; matrix products, arithmetic and copies ran while one was open for 34% of the time, Pallas kernels for 0%

profile of v1, /device:TPU:0, one launch (start us, length us, event | category | flops | bytes accessed | tf_op | source)
XLA Modules:
  0.0 247.6 jit_solution(2950720111783867780)
XLA Ops:
  7.2 0.0 copy-start
  7.2 0.0 copy-start.1
  7.2 0.8 compare_bitcast_fusion
  8.0 0.7 fusion.30
  8.7 0.7 and_select_fusion
  9.4 6.8 %gather_fusion.1 = s32[1024]{0:T(1024)S(1)} fusion(s32[256]{0:T(256)S(1)} %and_select_fusion, s32[1024]{0:T(1024)S(1)} %fusion.30), kind=kCustom, calls=%fused_computation.1 | custom fusion | bytes 12288 | tf_op jit(solution)/shard_map/gather | solution.py:75
  16.2 0.6 fusion.28
  16.8 5.2 %all-to-all-start.1 = ((bf16[8,128,8]{1,2,0:T(8,128)(2,1)}), bf16[8,128,8]{1,2,0:T(8,128)(2,1)S(1)}, u32[]{:S(2)}, u32[]{:S(2)}) async-start(bf16[8,128,8]{1,2,0:T(8,128)(2,1)} %fusion.28), calls=%async_computation.2 | async-start | bytes 32768 | tf_op jit(solution)/shard_map/all_to_all | solution.py:103
  22.0 5.1 %gather_fusion.2 = bf16[1024,512]{1,0:T(8,128)(2,1)} fusion(bf16[256,512]{1,0:T(8,128)(2,1)S(1)} %copy-done.1, s32[1024]{0:T(1024)S(1)} %fusion.30), kind=kCustom, calls=%fused_computation.2 | custom fusion | bytes 2101248 | tf_op jit(solution)/shard_map/gather | solution.py:81
  27.1 0.0 all-to-all-done.1
  27.1 4.2 %all-to-all-start.3 = ((bf16[8,128,512]{2,1,0:T(8,128)(2,1)}), bf16[8,128,512]{2,1,0:T(8,128)(2,1)S(1)}, u32[]{:S(2)}, u32[]{:S(2)}) async-start(bf16[8,128,512]{2,1,0:T(8,128)(2,1)} %bitcast.14), calls=%async_computation.4 | async-start | bytes 2097152 | tf_op jit(solution)/shard_map/all_to_all | solution.py:120
  31.3 0.0 copy-done
  31.3 6.0 %gather_fusion = bf16[1024,2048]{1,0:T(8,128)(2,1)} fusion(bf16[256,2048]{1,0:T(8,128)(2,1)S(1)} %copy-done, s32[1024]{0:T(1024)S(1)} %fusion.30), kind=kCustom, calls=%fused_computation | custom fusion | bytes 8392704 | tf_op jit(solution)/shard_map/gather | solution.py:80
  37.2 9.4 %all-to-all-done.3 = bf16[8,128,512]{2,1,0:T(8,128)(2,1)S(1)} async-done(((bf16[8,128,512]{2,1,0:T(8,128)(2,1)}), bf16[8,128,512]{2,1,0:T(8,128)(2,1)S(1)}, u32[]{:S(2)}, u32[]{:S(2)}) %all-to-all-start.3) | async-done | bytes 1048608 | tf_op jit(solution)/shard_map/all_to_all | solution.py:120
  46.7 4.7 %all-to-all-start = ((bf16[8,128,2048]{2,1,0:T(8,128)(2,1)}), bf16[8,128,2048]{2,1,0:T(8,128)(2,1)}, u32[]{:S(2)}, u32[]{:S(2)}) async-start(bf16[8,128,2048]{2,1,0:T(8,128)(2,1)} %bitcast.50), calls=%async_computation.1 | async-start | bytes 8388608 | tf_op jit(solution)/shard_map/all_to_all | solution.py:102
  51.4 0.0 all-gather.2.cloned.1.call-start
  51.4 0.7 all-gather.2.cloned.1.call-update
  52.2 0.7 multiply_reduce_fusion.1
  53.0 40.8 %all-reduce.1 = bf16[1024,128]{0,1:T(8,128)(2,1)S(1)} all-reduce(f32[1024,128]{0,1:T(8,128)S(1)} %constant_dynamic-update-slice_fusion), channel_id=1, replica_groups=mesh['fsdp'=4,'adapter'=8] {'fsdp'}, use_global_device_ids=true, to_apply=%region_4.5 | all-reduce | flops 131072 | bytes 786432 | tf_op jit(solution)/shard_map/psum | solution.py:122
  93.9 8.3 %fusion.2 = bf16[1024,2048]{1,0:T(8,128)(2,1)} fusion(bf16[8,2048,128]{2,1,0:T(8,128)(2,1)} %param.11, bf16[1024,8]{0,1:T(8,128)(2,1)S(1)} %bitcast.56, bf16[1024,128]{0,1:T(8,128)(2,1)S(1)} %all-reduce.1), kind=kOutput, calls=%fused_computation.8 | convolution fusion | flops 4300210176 | bytes 8667136 | tf_op jit(solution)/shard_map/wnr,nyr->wy/dot_general | solution.py:47
  102.2 0.0 all-to-all-done
  102.2 4.5 %all-to-all-start.4 = ((bf16[8,128,2048]{2,1,0:T(8,128)(2,1)}), bf16[8,128,2048]{2,1,0:T(8,128)(2,1)}, u32[]{:S(2)}, u32[]{:S(2)}) async-start(bf16[8,128,2048]{2,1,0:T(8,128)(2,1)} %bitcast.51), calls=%async_computation.5 | async-start | bytes 8388608 | tf_op jit(solution)/shard_map/all_to_all | solution.py:133
  106.8 0.2 reduce-scatter.2.cloned.1.call-start
  107.0 7.2 %fusion.32 = f32[2048,256]{1,0:T(8,128)} fusion(bf16[2048,2048]{1,0:T(8,128)(2,1)} %param.10, bf16[256,2048]{1,0:T(8,128)(2,1)S(1)} %copy-done), kind=kOutput, calls=%fused_computation.50 | convolution fusion | flops 2147483648 | bytes 11534336 | tf_op jit(solution)/shard_map/dot_general | solution.py:87
  114.2 0.0 reduce-scatter.2.cloned.1.call-update
  114.2 0.0 copy-start.3
  114.2 7.6 %multiply_reduce_fusion = f32[1024,128]{1,0:T(8,128)S(1)} fusion(bf16[1024,2048,1]{1,0,2:T(8,128)(2,1)} %bitcast.7, bf16[8,2048,128]{2,1,0:T(8,128)(2,1)} %param.11, f32[1024,8]{0,1:T(8,128)S(1)} %bitcast_convert_fusion), kind=kOutput, calls=%fused_computation.10 | convolution fusion | flops 4296933376 | bytes 8945664 | tf_op jit(solution)/shard_map/sd,ldk->slk/dot_general | solution.py:20
  121.8 0.1 collective-permute-start
  121.9 36.5 %collective-permute-done = f32[1024,128]{1,0:T(8,128)S(1)} collective-permute-done((f32[1024,128]{1,0:T(8,128)S(1)}, f32[1024,128]{1,0:T(8,128)S(1)}, u32[]{:S(2)}, u32[]{:S(2)}) %collective-permute-start) | collective-permute-done | bytes 524320 | tf_op jit(solution)/shard_map/ppermute | solution.py:14
  158.4 0.1 add.55
  158.5 0.1 collective-permute-start.1
  158.5 0.0 all-gather.2.cloned.1.call-done
  158.6 7.5 %fusion.33 = f32[256,2048]{1,0:T(8,128)} fusion(bf16[256,2048]{1,0:T(8,128)(2,1)} %all-gather.2.cloned.1.call-done, bf16[2048,2048]{1,0:T(8,128)(2,1)} %param.10), kind=kOutput, calls=%fused_computation.51 | convolution fusion | flops 2147483648 | bytes 11534336 | tf_op jit(solution)/shard_map/dot_general | solution.py:95
  166.0 22.1 %collective-permute-done.1 = f32[1024,128]{1,0:T(8,128)S(1)} collective-permute-done((f32[1024,128]{1,0:T(8,128)S(1)}, f32[1024,128]{1,0:T(8,128)S(1)}, u32[]{:S(2)}, u32[]{:S(2)}) %collective-permute-start.1) | collective-permute-done | bytes 524320 | tf_op jit(solution)/shard_map/ppermute | solution.py:14
  188.2 0.3 fusion.22
  188.5 0.1 copy.17
  188.6 1.8 fusion.8
  190.4 0.0 all-to-all-done.4
  190.4 3.8 %all-to-all-start.2 = ((bf16[8,128,512]{2,1,0:T(8,128)(2,1)}), bf16[8,128,512]{2,1,0:T(8,128)(2,1)S(1)}, u32[]{:S(2)}, u32[]{:S(2)}) async-start(bf16[8,128,512]{2,1,0:T(8,128)(2,1)} %bitcast.12), calls=%async_computation.3 | async-start | bytes 2097152 | tf_op jit(solution)/shard_map/all_to_all | solution.py:113
  194.2 8.2 %fusion.3 = bf16[8,2048,128]{1,2,0:T(8,128)(2,1)} fusion(bf16[1024,2048,1]{1,0,2:T(8,128)(2,1)} %bitcast.7, bf16[1024,8]{0,1:T(8,128)(2,1)S(1)} %bitcast.58, bf16[1024,128]{0,1:T(8,128)(2,1)S(1)} %all-reduce.1), kind=kOutput, calls=%fused_computation.11 | convolution fusion | flops 4300210176 | bytes 8667136 | tf_op jit(solution)/shard_map/wq,wmu->mqu/dot_general | solution.py:50
  202.4 6.4 %copy.20 = bf16[8,2048,128]{2,1,0:T(8,128)(2,1)} copy(bf16[8,2048,128]{1,2,0:T(8,128)(2,1)} %fusion.3) | data formatting | bytes 8388608
  208.8 1.2 copy.18
  210.1 17.5 %scatter_custom_fusion.1 = f32[256,2048]{1,0:T(8,128)} fusion(f32[256,2048]{1,0:T(8,128)} %fusion.33, s32[1024]{0:T(1024)S(1)} %bitcast.62, bf16[1024,2048]{1,0:T(8,128)(2,1)} %bitcast.24), kind=kCustom, calls=%fused_computation.5 | custom fusion | flops 4194304 | bytes 6291456 | tf_op jit(solution)/shard_map/scatter-add | solution.py:149
  227.6 2.7 %convert_element_type.60 = bf16[256,2048]{1,0:T(8,128)(2,1)} convert(f32[256,2048]{1,0:T(8,128)} %scatter_custom_fusion.1) | non-fusion elementwise | flops 524288 | bytes 3145728 | tf_op jit(solution)/shard_map/convert_element_type | solution.py:151
  230.3 2.7 %fusion.15 = bf16[8,64,512]{2,1,0:T(8,128)(2,1)} fusion(bf16[1024,512,1]{1,0,2:T(8,128)(2,1)} %bitcast.54, bf16[1024,8]{0,1:T(8,128)(2,1)S(1)} %bitcast.59, bf16[1024,64]{0,1:T(8,128)(2,1)S(1)} %copy.17), kind=kOutput, calls=%fused_computation.23 | convolution fusion | flops 537919488 | bytes 1720320 | tf_op jit(solution)/shard_map/slr,sc->lrc/dot_general | solution.py:53
  233.0 0.0 all-to-all-done.2
  233.0 6.9 %scatter_custom_fusion = f32[256,512]{1,0:T(8,128)S(1)} fusion(f32[256,512]{1,0:T(8,128)S(1)} %copy.18, s32[1024]{0:T(1024)S(1)} %bitcast.63, bf16[1024,512]{1,0:T(8,128)(2,1)S(1)} %bitcast.52), kind=kCustom, calls=%fused_computation.14 | custom fusion | flops 1048576 | bytes 1572864 | tf_op jit(solution)/shard_map/scatter-add | solution.py:143
  240.0 0.7 convert_element_type.55
  (11 shorter events, 0.1 us)
Async XLA Ops:
  7.2 24.1 %copy-start = (bf16[256,2048]{1,0:T(8,128)(2,1)S(1)}, bf16[256,2048]{1,0:T(8,128)(2,1)}, u32[]{:S(2)}) copy-start(bf16[256,2048]{1,0:T(8,128)(2,1)} %param.7) | copy-start | bytes 3145732
  7.2 14.8 %copy-start.1 = (bf16[256,512]{1,0:T(8,128)(2,1)S(1)}, bf16[256,512]{1,0:T(8,128)(2,1)}, u32[]{:S(2)}) copy-start(bf16[256,512]{1,0:T(8,128)(2,1)} %param.13) | copy-start | bytes 786436
  16.8 10.3 %all-to-all-start.1 = ((bf16[8,128,8]{1,2,0:T(8,128)(2,1)}), bf16[8,128,8]{1,2,0:T(8,128)(2,1)S(1)}, u32[]{:S(2)}, u32[]{:S(2)}) async-start(bf16[8,128,8]{1,2,0:T(8,128)(2,1)} %fusion.28), calls=%async_computation.2 | async-start | bytes 32768 | tf_op jit(solution)/shard_map/all_to_all | solution.py:103
  27.1 19.6 %all-to-all-start.3 = ((bf16[8,128,512]{2,1,0:T(8,128)(2,1)}), bf16[8,128,512]{2,1,0:T(8,128)(2,1)S(1)}, u32[]{:S(2)}, u32[]{:S(2)}) async-start(bf16[8,128,512]{2,1,0:T(8,128)(2,1)} %bitcast.14), calls=%async_computation.4 | async-start | bytes 2097152 | tf_op jit(solution)/shard_map/all_to_all | solution.py:120
  46.7 5.5 %copy-start.2 = (bf16[8,128,512]{2,1,0:T(8,128)(2,1)}, bf16[8,128,512]{2,1,0:T(8,128)(2,1)S(1)}, u32[]{:S(2)}) copy-start(bf16[8,128,512]{2,1,0:T(8,128)(2,1)S(1)} %all-to-all-done.3) | copy-start | bytes 3145732
  46.7 5.5 %copy-start.4 = (bf16[8,64,512]{2,1,0:T(8,128)(2,1)S(1)}, bf16[8,64,512]{2,1,0:T(8,128)(2,1)}, u32[]{:S(2)}) copy-start(bf16[8,64,512]{2,1,0:T(8,128)(2,1)} %param.12) | copy-start | bytes 1572868
  46.7 55.5 %all-to-all-start = ((bf16[8,128,2048]{2,1,0:T(8,128)(2,1)}), bf16[8,128,2048]{2,1,0:T(8,128)(2,1)}, u32[]{:S(2)}, u32[]{:S(2)}) async-start(bf16[8,128,2048]{2,1,0:T(8,128)(2,1)} %bitcast.50), calls=%async_computation.1 | async-start | bytes 8388608 | tf_op jit(solution)/shard_map/all_to_all | solution.py:102
  51.4 107.2 %all-gather.2.cloned.1.call-start = ((), (), s32[]{:S(2)}) async-start(), calls=%async_computation.7 | async-start | bytes 1310720 | tf_op jit(solution)/shard_map/all_gather | solution.py:96
  102.2 88.2 %all-to-all-start.4 = ((bf16[8,128,2048]{2,1,0:T(8,128)(2,1)}), bf16[8,128,2048]{2,1,0:T(8,128)(2,1)}, u32[]{:S(2)}, u32[]{:S(2)}) async-start(bf16[8,128,2048]{2,1,0:T(8,128)(2,1)} %bitcast.51), calls=%async_computation.5 | async-start | bytes 8388608 | tf_op jit(solution)/shard_map/all_to_all | solution.py:133
  106.8 102.1 %reduce-scatter.2.cloned.1.call-start = ((), (), s32[]{:S(2)}) async-start(), calls=%async_computation.6 | async-start | bytes 2621440 | tf_op jit(solution)/shard_map/reduce_scatter | solution.py:86
  114.2 7.7 %copy-start.3 = (s32[1,8,128]{2,1,0:T(8,128)S(1)}, s32[1,8,128]{2,1,0:T(8,128)}, u32[]{:S(2)}) copy-start(s32[1,8,128]{2,1,0:T(8,128)} %param.9) | copy-start | bytes 12292
  121.8 36.6 %collective-permute-start = (f32[1024,128]{1,0:T(8,128)S(1)}, f32[1024,128]{1,0:T(8,128)S(1)}, u32[]{:S(2)}, u32[]{:S(2)}) collective-permute-start(f32[1024,128]{1,0:T(8,128)S(1)} %multiply_reduce_fusion), channel_id=1, source_target_pairs={{0,8},{8,0},{16,24},{24,16},{1,9},{9,1},{17,25},{25,17},{2,10},{10... | collective-permute-start | bytes 1572872 | tf_op jit(solution)/shard_map/ppermute | solution.py:14
  158.5 29.7 %collective-permute-start.1 = (f32[1024,128]{1,0:T(8,128)S(1)}, f32[1024,128]{1,0:T(8,128)S(1)}, u32[]{:S(2)}, u32[]{:S(2)}) collective-permute-start(f32[1024,128]{1,0:T(8,128)S(1)} %add.55), channel_id=1, source_target_pairs={{0,16},{8,24},{16,0},{24,8},{1,17},{9,25},{17,1},{25,9},{2,18},{10... | collective-permute-start | bytes 1572872 | tf_op jit(solution)/shard_map/ppermute | solution.py:14
  190.4 42.6 %all-to-all-start.2 = ((bf16[8,128,512]{2,1,0:T(8,128)(2,1)}), bf16[8,128,512]{2,1,0:T(8,128)(2,1)S(1)}, u32[]{:S(2)}, u32[]{:S(2)}) async-start(bf16[8,128,512]{2,1,0:T(8,128)(2,1)} %bitcast.12), calls=%async_computation.3 | async-start | bytes 2097152 | tf_op jit(solution)/shard_map/all_to_all | solution.py:113
Sparse Core Ops, SparseCore 0:
  53.8 40.9 all-gather.1
  114.3 62.0 reduce-scatter.1
